TPU v7x, 256 devices: a whole 4x4x8 slice. The times are simulated.
256 devices in a mesh: spec: 4 (over x), geo: 64 (over y, z, core).
Axes of the slice: x: 4, y: 4, z: 8, core: 2. Of those that a mesh axis runs over, the one named last changes fastest.
Arguments:
- spectrum: bfloat16 [1296, 1024, 128], P('spec', 'geo'), may hold values from 0.01 to 11, as said below
- sea_map: int32 [1024, 128], P('geo'), may hold values 0 or 1
- depth_factor: float32 [1024, 128], P('geo'), may hold values from 0.25 to 1
- wind_speed: bfloat16 [1024, 128], P('geo'), may hold values from 0.19921875 to 2
- wind_dir: bfloat16 [1024, 128], P('geo'), may hold values from -3.140625 to 3.140625
- ice_mask: int32 [1024, 128], P('geo'), may hold values from 0 to 1, as said below
- owner_map: int32 [1024, 128], P('geo'), may hold values from 0 to 63, as said below
- pair_kernel: bfloat16 [1296, 1296], replicated, may hold values from -1 to 2
- transfer_kernel: bfloat16 [64, 1296, 1296], P('geo'), may hold values from -1 to 2
Outputs:
- updated: bfloat16 [1296, 1024, 128], P('spec', 'geo')
Inputs may be any that keep to these rules, and one draw needn't show every extreme that they name: `owner_map`: in each aligned block of 512 cells of the grid in row-major order, no owner is named by more than 16 cells, and one owner, the same in every block, is named by exactly 16 cells of each block. `ice_mask`: 1 marks ice. Cells of the owner that is named by 16 cells of every block are free of ice. `spectrum`: Positive.
All inputs are finite; a program needn't handle non-finite values. No bound on the sum of `sea_map` on one device may be relied on, other than what follows from the above.
Results may differ from a plain program's by a relative error of at most 0.0059.
Values may be sent and summed in bfloat16 or wider, within the bound.
A program may use at most 64 MiB of HBM per device.

v0:
```python
import math

import jax
import jax.numpy as jnp
from jax import lax
from jax.sharding import PartitionSpec as P

NDIR = 36


def padded_2(cells, sides, width):
    for axis, dim in sides:
        count = lax.axis_size(axis)
        ends = count - 1
        head = lax.slice_in_dim(cells, 0, width, axis=dim)
        tail = lax.slice_in_dim(cells, cells.shape[dim] - width, cells.shape[dim], axis=dim)
        cells = jnp.concatenate(
            [
                lax.ppermute(tail, axis, [(i, (i + 1) % count) for i in range(ends)]),
                cells,
                lax.ppermute(head, axis, [((i + 1) % count, i) for i in range(ends)]),
            ],
            axis=dim,
        )
    return cells


def finish(row_data, transfer, wind_rows, wind_angle):
    energy = row_data.astype(jnp.float32)
    total = jnp.mean(energy, axis=0)
    ratio = total / (1.0 + total)
    component = jnp.arange(row_data.shape[0], dtype=jnp.int32)
    heading = 2.0 * math.pi * ((component % NDIR).astype(jnp.float32) + 0.5) / NDIR
    forcing = (
        0.3
        * wind_rows.astype(jnp.float32)[None, :]
        * jnp.maximum(jnp.cos(heading[:, None] - wind_angle.astype(jnp.float32)[None, :]), 0.0)
    )
    result = (
        energy * (1.0 + forcing - 0.5 * ratio[None, :])
        + 0.2 * transfer.astype(jnp.float32) / (1.0 + total)[None, :]
    )
    return result.astype(jnp.bfloat16)


def pair_up(pair_kernel, row_data):
    coupled = jnp.dot(pair_kernel, row_data, preferred_element_type=jnp.float32)
    return (row_data.astype(jnp.float32) * coupled).astype(jnp.bfloat16)


def per_device(
    spectrum,
    sea_map,
    depth_factor,
    wind_speed,
    wind_dir,
    ice_mask,
    owner_map,
    pair_kernel,
    transfer_kernel,
):
    comp_dev, cells_x, cells_y = spectrum.shape
    spec_count = lax.axis_size("spec")
    geo_count = lax.axis_size("geo")
    rows_dev = cells_x * cells_y // spec_count
    capacity = 2 * rows_dev // geo_count
    slot_count = geo_count * capacity
    masked = spectrum * sea_map.astype(jnp.bfloat16)[None, :, :]
    padded = padded_2(masked, (("geo", 1),), 1)
    extended = padded.astype(jnp.float32)
    component = lax.axis_index("spec") * comp_dev + jnp.arange(comp_dev, dtype=jnp.int32)
    frequency = (component // NDIR).astype(jnp.float32)
    heading = 2.0 * math.pi * ((component % NDIR).astype(jnp.float32) + 0.5) / NDIR
    cosine = jnp.cos(heading)[:, None, None]
    sine = jnp.sin(heading)[:, None, None]
    gain = (jnp.float32(1.1) ** (-0.5 * frequency))[:, None, None]
    sea_weight = sea_map.astype(jnp.float32)
    step_x = 0.7 * gain * jnp.abs(cosine) * depth_factor
    step_y = 0.7 * gain * jnp.abs(sine) * depth_factor
    centre = extended[:, 1:-1]
    west_side = extended[:, :-2]
    east_side = extended[:, 2:]
    zeros_y = jnp.zeros((comp_dev, cells_x, 1), jnp.float32)
    south_side = jnp.concatenate([zeros_y, centre[:, :, :-1]], axis=2)
    north_side = jnp.concatenate([centre[:, :, 1:], zeros_y], axis=2)
    upwind_x = jnp.where(cosine > 0, west_side, east_side)
    upwind_y = jnp.where(sine > 0, south_side, north_side)
    advected = centre - step_x * (centre - upwind_x) - step_y * (centre - upwind_y)
    propagated = (advected * sea_weight).astype(jnp.bfloat16)
    flattened = propagated.reshape(comp_dev, cells_x * cells_y)
    row_data = lax.all_to_all(flattened, "spec", split_axis=1, concat_axis=0, tiled=True)
    offset = lax.axis_index("spec") * rows_dev

    def own_rows(values):
        return lax.dynamic_slice_in_dim(values.reshape(-1), offset, rows_dev)

    owners = own_rows(owner_map)
    is_live = 1 - own_rows(ice_mask)
    wind_rows = own_rows(wind_speed)
    wind_angle = own_rows(wind_dir)
    onehot = (owners[:, None] == jnp.arange(geo_count, dtype=jnp.int32)[None, :]).astype(
        jnp.int32
    ) * is_live[:, None]
    before = jnp.cumsum(onehot, axis=0) - onehot
    position = jnp.sum(before * onehot, axis=1)
    slot_index = jnp.where(is_live == 1, owners * capacity + position, slot_count)
    source = (
        jnp.full((slot_count,), rows_dev, jnp.int32)
        .at[slot_index]
        .set(jnp.arange(rows_dev, dtype=jnp.int32), mode="drop")
    )
    filled = source < rows_dev
    source_clip = jnp.minimum(source, rows_dev - 1)
    slot_clip = jnp.minimum(slot_index, slot_count - 1)

    def to_slots(values):
        return jnp.where(
            filled[None, :], jnp.take(values, source_clip, axis=1), jnp.zeros((), values.dtype)
        )

    own_kernel = transfer_kernel[0]
    outgoing = to_slots(row_data)
    wind_slots = to_slots(jnp.stack([wind_rows, wind_angle]))
    arrived, arrived_wind = (
        lax.all_to_all(outgoing, "geo", split_axis=1, concat_axis=1, tiled=True),
        lax.all_to_all(wind_slots, "geo", split_axis=1, concat_axis=1, tiled=True),
    )
    paired = pair_up(pair_kernel, arrived)
    transfer = jnp.dot(own_kernel, paired, preferred_element_type=jnp.float32).astype(jnp.bfloat16)
    sourced = finish(arrived, transfer, arrived_wind[0], arrived_wind[1])
    returned = lax.all_to_all(sourced, "geo", split_axis=1, concat_axis=1, tiled=True)
    result = jnp.where(is_live[None, :] == 1, jnp.take(returned, slot_clip, axis=1), row_data)
    restored = lax.all_to_all(result, "spec", split_axis=0, concat_axis=1, tiled=True)
    return restored.reshape(comp_dev, cells_x, cells_y)


def solution(mesh):
    placed = (
        P("spec", "geo", None),
        P("geo", None),
        P("geo", None),
        P("geo", None),
        P("geo", None),
        P("geo", None),
        P("geo", None),
        P(),
        P("geo", None, None),
    )
    return jax.shard_map(
        per_device, mesh=mesh, in_specs=placed, out_specs=P("spec", "geo", None), check_vma=False
    )
```

profile of v0, /device:TPU:1, one launch (start us, length us, event | category | flops | bytes accessed | tf_op | source)
XLA Modules:
  0.0 282.3 jit_solution(1585791736908418850)
XLA Ops:
  0.8 1.7 copy_multiply_fusion
  2.5 5.1 %collective-permute-start.1 = (bf16[324,1,128]{2,0,1:T(8,128)(2,1)S(1)}, bf16[324,1,128]{2,0,1:T(8,128)(2,1)S(1)}, u32[]{:S(2)}, u32[]{:S(2)}) collective-permute-start(bf16[324,1,128]{2,0,1:T(8,128)(2,1)S(1)} %get-tuple-element.13), channel_id=1, source_target_pairs={{1,0},{2,1},{3,2},{4,3},{5,4},{6,5},{7,6},{8,7},{9,8},{10,9},{11,1... | collective-permute-start | bytes 248840 | tf_op jit(solution)/shard_map/ppermute | solution.py:21
  7.6 1.9 collective-permute-start
  12.9 1.9 fusion.9
  16.9 3.8 %all-to-all-start = ((bf16[324,4,512]{2,0,1:T(8,128)(2,1)}), bf16[324,4,512]{2,0,1:T(8,128)(2,1)S(1)}, u32[]{:S(2)}, u32[]{:S(2)}) async-start(bf16[324,4,512]{2,0,1:T(8,128)(2,1)} %copy.35), calls=%async_computation | async-start | bytes 2686976 | tf_op jit(solution)/shard_map/all_to_all | solution.py:91
  20.7 2.4 scatter_custom_fusion
  25.1 3.2 %gather_fusion.1 = bf16[1024,2]{1,0:T(8,128)(2,1)S(1)} fusion(bf16[2,512]{0,1:T(8,128)(2,1)S(1)} %copy.38, s32[1024]{0:T(1024)S(1)} %fusion.21), kind=kCustom, calls=%fused_computation.1 | custom fusion | bytes 12288 | tf_op jit(solution)/shard_map/jit(_take)/gather | solution.py:118
  29.5 9.3 %all-to-all-done = bf16[324,4,512]{2,0,1:T(8,128)(2,1)S(1)} async-done(((bf16[324,4,512]{2,0,1:T(8,128)(2,1)}), bf16[324,4,512]{2,0,1:T(8,128)(2,1)S(1)}, u32[]{:S(2)}, u32[]{:S(2)}) %all-to-all-start) | async-done | bytes 1327136 | tf_op jit(solution)/shard_map/all_to_all | solution.py:91
  38.8 12.4 %all-to-all-start.2 = ((bf16[2,64,16]{2,0,1:T(2,128)(2,1)}), bf16[2,64,16]{2,0,1:T(2,128)(2,1)S(1)}, u32[]{:S(2)}, u32[]{:S(2)}) async-start(bf16[2,64,16]{2,0,1:T(2,128)(2,1)} %broadcast_select_fusion.1), calls=%async_computation.2 | async-start | bytes 65536 | tf_op jit(solution)/shard_map/all_to_all | solution.py:126
  52.4 5.5 %gather_fusion = bf16[1024,1296]{1,0:T(8,128)(2,1)} fusion(bf16[1296,512]{0,1:T(8,128)(2,1)S(1)} %copy.36, s32[1024]{0:T(1024)S(1)} %fusion.21), kind=kCustom, calls=%fused_computation | custom fusion | bytes 5312512 | tf_op jit(solution)/shard_map/jit(_take)/gather | solution.py:118
  57.9 3.3 %select_select_fusion = bf16[1296,64,16]{0,2,1:T(8,128)(2,1)} fusion(bf16[1296,64,16]{0,2,1:T(8,128)(2,1)} %bitcast.76, pred[64,16]{1,0:T(8,128)(4,1)S(1)} %broadcast_in_dim.115, pred[64,16]{1,0:T(8,128)(4,1)S(1)} %broadcast_in_dim.113), kind=kLoop, calls=%fused_computation.12 | loop fusion | flops 2654208 | bytes 5310464 | tf_op jit(solution)/shard_map/jit(_where)/select_n | solution.py:117
  61.2 10.3 %all-to-all-start.1 = ((bf16[1296,64,16]{0,2,1:T(8,128)(2,1)}), bf16[1296,64,16]{0,2,1:T(8,128)(2,1)S(1)}, u32[]{:S(2)}, u32[]{:S(2)}) async-start(bf16[1296,64,16]{0,2,1:T(8,128)(2,1)} %select_select_fusion), calls=%async_computation.1 | async-start | bytes 5767168 | tf_op jit(solution)/shard_map/all_to_all | solution.py:125
  71.9 67.5 %all-to-all-done.1 = bf16[1296,64,16]{0,2,1:T(8,128)(2,1)S(1)} async-done(((bf16[1296,64,16]{0,2,1:T(8,128)(2,1)}), bf16[1296,64,16]{0,2,1:T(8,128)(2,1)S(1)}, u32[]{:S(2)}, u32[]{:S(2)}) %all-to-all-start.1) | async-done | bytes 2654240 | tf_op jit(solution)/shard_map/all_to_all | solution.py:125
  139.4 2.8 copy.37
  142.8 7.1 %fusion.58 = bf16[1296,1024]{1,0:T(8,128)(2,1)S(1)} fusion(bf16[1296,1296]{1,0:T(8,128)(2,1)} %param.16, bf16[1296,1024]{0,1:T(8,128)(2,1)S(1)} %bitcast.73, bf16[1296,1024]{1,0:T(8,128)(2,1)} %copy.37), kind=kOutput, calls=%bitcast_fusion.1.clone.1 | convolution fusion | flops 3443834880 | bytes 11321856 | tf_op jit(solution)/shard_map/dot_general | solution.py:47
  149.9 22.4 %fusion.1 = bf16[1296,1024]{1,0:T(8,128)(2,1)S(1)} fusion(bf16[1296,1024]{1,0:T(8,128)(2,1)S(1)} %copy-done.2, bf16[1,1296,1296]{2,1,0:T(8,128)(2,1)S(1)} %copy-done.6, f32[1024]{0:T(1024)S(1)} %get-tuple-element.17, f32[1024]{0:T(1024)S(1)} %get-tuple-element.16, f32[1024]{0:T(1024)S(1)} %reshape.197, f32[1296]{0:T(1024)S(1)} %fusion.17, ...), kind=kOutput, calls=%fused_computation.8 | convolution fusion | flops 3457105920 | bytes 11343424 | tf_op jit(solution)/shard_map/dot_general | solution.py:129
  172.3 2.9 %copy.40 = bf16[1296,1024]{0,1:T(8,128)(2,1)} copy(bf16[1296,1024]{1,0:T(8,128)(2,1)S(1)} %fusion.1) | data formatting | bytes 5308416 | tf_op jit(solution)/shard_map/convert_element_type | solution.py:43
  175.2 5.7 %all-to-all-start.3 = ((bf16[1296,64,16]{0,2,1:T(8,128)(2,1)}), bf16[1296,64,16]{0,2,1:T(8,128)(2,1)S(1)}, u32[]{:S(2)}, u32[]{:S(2)}) async-start(bf16[1296,64,16]{0,2,1:T(8,128)(2,1)} %bitcast.75), calls=%async_computation.3 | async-start | bytes 5767168 | tf_op jit(solution)/shard_map/all_to_all | solution.py:131
  181.0 67.9 %all-to-all-done.3 = bf16[1296,64,16]{0,2,1:T(8,128)(2,1)S(1)} async-done(((bf16[1296,64,16]{0,2,1:T(8,128)(2,1)}), bf16[1296,64,16]{0,2,1:T(8,128)(2,1)S(1)}, u32[]{:S(2)}, u32[]{:S(2)}) %all-to-all-start.3) | async-done | bytes 2654240 | tf_op jit(solution)/shard_map/all_to_all | solution.py:131
  248.8 2.9 %gather_fusion.2 = bf16[512,1296]{1,0:T(8,128)(2,1)} fusion(bf16[1296,1024]{0,1:T(8,128)(2,1)S(1)} %bitcast.71, s32[1024]{0:T(1024)S(1)} %pad_clamp_fusion), kind=kCustom, calls=%fused_computation.2 | custom fusion | bytes 2656256 | tf_op jit(solution)/shard_map/jit(_take)/gather | solution.py:132
  251.7 3.8 %reshape.234 = bf16[4,324,512]{1,0,2:T(4,128)(2,1)S(1)} reshape(bf16[1296,512]{0,1:T(8,128)(2,1)} %bitcast.78) | data formatting | bytes 2654208 | tf_op jit(solution)/shard_map/jit(_take)/gather | solution.py:132
  255.5 2.5 copy.43
  258.0 1.5 select_select_fusion.1
  259.4 20.8 %all_to_all.59 = bf16[4,324,512]{2,1,0:T(8,128)(2,1)S(1)} all-to-all(bf16[4,324,512]{2,1,0:T(8,128)(2,1)S(1)} %select_select_fusion.1), channel_id=1, replica_groups=mesh['spec'=4,'geo'=64] {'spec'}, dimensions={0} | all-to-all | bytes 2654208 | tf_op jit(solution)/shard_map/all_to_all | solution.py:133
  (64 shorter events, 13.4 us)
Async XLA Ops:
  0.0 9.6 %copy-start.5 = (s32[16,128]{1,0:T(8,128)S(1)}, s32[16,128]{1,0:T(8,128)}, u32[]{:S(2)}) copy-start(s32[16,128]{1,0:T(8,128)} %param.14) | copy-start | bytes 24580
  0.0 9.7 %copy-start.4 = (s32[16,128]{1,0:T(8,128)S(1)}, s32[16,128]{1,0:T(8,128)}, u32[]{:S(2)}) copy-start(s32[16,128]{1,0:T(8,128)} %param.15) | copy-start | bytes 24580
  2.5 9.2 %collective-permute-start.1 = (bf16[324,1,128]{2,0,1:T(8,128)(2,1)S(1)}, bf16[324,1,128]{2,0,1:T(8,128)(2,1)S(1)}, u32[]{:S(2)}, u32[]{:S(2)}) collective-permute-start(bf16[324,1,128]{2,0,1:T(8,128)(2,1)S(1)} %get-tuple-element.13), channel_id=1, source_target_pairs={{1,0},{2,1},{3,2},{4,3},{5,4},{6,5},{7,6},{8,7},{9,8},{10,9},{11,1... | collective-permute-start | bytes 248840 | tf_op jit(solution)/shard_map/ppermute | solution.py:21
  7.6 4.1 %collective-permute-start = (bf16[324,1,128]{2,0,1:T(8,128)(2,1)S(1)}, bf16[324,1,128]{2,0,1:T(8,128)(2,1)S(1)}, u32[]{:S(2)}, u32[]{:S(2)}) collective-permute-start(bf16[324,1,128]{2,0,1:T(8,128)(2,1)S(1)} %get-tuple-element.12), channel_id=1, source_target_pairs={{0,1},{1,2},{2,3},{3,4},{4,5},{5,6},{6,7},{7,8},{8,9},{9,10},{10,1... | collective-permute-start | bytes 248840 | tf_op jit(solution)/shard_map/ppermute | solution.py:19
  12.0 0.9 copy-start.3
  16.9 22.0 %all-to-all-start = ((bf16[324,4,512]{2,0,1:T(8,128)(2,1)}), bf16[324,4,512]{2,0,1:T(8,128)(2,1)S(1)}, u32[]{:S(2)}, u32[]{:S(2)}) async-start(bf16[324,4,512]{2,0,1:T(8,128)(2,1)} %copy.35), calls=%async_computation | async-start | bytes 2686976 | tf_op jit(solution)/shard_map/all_to_all | solution.py:91
  38.8 12.4 %copy-start = (bf16[324,4,512]{2,0,1:T(8,128)(2,1)}, bf16[324,4,512]{2,0,1:T(8,128)(2,1)S(1)}, u32[]{:S(2)}) copy-start(bf16[324,4,512]{2,0,1:T(8,128)(2,1)S(1)} %all-to-all-done) | copy-start | bytes 3981316
  38.8 22.4 %all-to-all-start.2 = ((bf16[2,64,16]{2,0,1:T(2,128)(2,1)}), bf16[2,64,16]{2,0,1:T(2,128)(2,1)S(1)}, u32[]{:S(2)}, u32[]{:S(2)}) async-start(bf16[2,64,16]{2,0,1:T(2,128)(2,1)} %broadcast_select_fusion.1), calls=%async_computation.2 | async-start | bytes 65536 | tf_op jit(solution)/shard_map/all_to_all | solution.py:126
  61.2 78.2 %all-to-all-start.1 = ((bf16[1296,64,16]{0,2,1:T(8,128)(2,1)}), bf16[1296,64,16]{0,2,1:T(8,128)(2,1)S(1)}, u32[]{:S(2)}, u32[]{:S(2)}) async-start(bf16[1296,64,16]{0,2,1:T(8,128)(2,1)} %select_select_fusion), calls=%async_computation.1 | async-start | bytes 5767168 | tf_op jit(solution)/shard_map/all_to_all | solution.py:125
  142.7 7.2 %copy-start.2 = (bf16[1296,1024]{1,0:T(8,128)(2,1)S(1)}, bf16[1296,1024]{1,0:T(8,128)(2,1)}, u32[]{:S(2)}) copy-start(bf16[1296,1024]{1,0:T(8,128)(2,1)} %copy.37) | copy-start | bytes 7962628
  142.7 7.2 %copy-start.6 = (bf16[1,1296,1296]{2,1,0:T(8,128)(2,1)S(1)}, bf16[1,1296,1296]{2,1,0:T(8,128)(2,1)}, u32[]{:S(2)}) copy-start(bf16[1,1296,1296]{2,1,0:T(8,128)(2,1)} %param.17) | copy-start | bytes 10077700
  175.2 73.6 %all-to-all-start.3 = ((bf16[1296,64,16]{0,2,1:T(8,128)(2,1)}), bf16[1296,64,16]{0,2,1:T(8,128)(2,1)S(1)}, u32[]{:S(2)}, u32[]{:S(2)}) async-start(bf16[1296,64,16]{0,2,1:T(8,128)(2,1)} %bitcast.75), calls=%async_computation.3 | async-start | bytes 5767168 | tf_op jit(solution)/shard_map/all_to_all | solution.py:131
  251.7 6.2 %copy-start.1 = (bf16[324,4,512]{2,0,1:T(8,128)(2,1)S(1)}, bf16[324,4,512]{2,0,1:T(8,128)(2,1)}, u32[]{:S(2)}) copy-start(bf16[324,4,512]{2,0,1:T(8,128)(2,1)} %copy-done) | copy-start | bytes 3981316
where the time goes:
time: 283 us; the launch traced here: 282 us
  waiting for transfers between devices  145 us (51%)
  starting transfers between devices  39.3 us (14%)
  local copies, waits for them, and re-layouts  35 us (12%)
  matrix products  29.5 us (10%)
  blocking collectives  20.8 us (7%)
  other arithmetic  12.6 us (4%)
    all_to_all x1, waiting for transfers between devices, per_device(): lax.all_to_all(sourced, 'geo', split_axis=1, concat_axis=1, tiled=True)  67.9 us
    all_to_all x1, waiting for transfers between devices, per_device(): lax.all_to_all(outgoing, 'geo', split_axis=1, concat_axis=1, tiled=True)  67.5 us
    dot_general x1, matrix products, per_device(): jnp.dot(own_kernel, paired, preferred_element_type=jnp.float32)  22.4 us
    all_to_all x1, blocking collectives, per_device(): lax.all_to_all(result, 'spec', split_axis=0, concat_axis=1, tiled=True)  20.8 us
    all_to_all x1, starting transfers between devices, per_device(): lax.all_to_all(wind_slots, 'geo', split_axis=1, concat_axis=1, tiled=True)  12.4 us
    all_to_all x1, starting transfers between devices, per_device(): lax.all_to_all(outgoing, 'geo', split_axis=1, concat_axis=1, tiled=True)  10.3 us
    all_to_all x1, waiting for transfers between devices, per_device(): lax.all_to_all(flattened, 'spec', split_axis=1, concat_axis=0, tiled=True)  9.32 us
    gather x3, local copies, waits for them, and re-layouts, to_slots(): jnp.take(values, source_clip, axis=1)  9.2 us
  transfers between devices with their start and end apart: 6, of which 3 were waited for; matrix products, arithmetic and copies ran while one was open for 7% of the time, Pallas kernels for 0%

commit v1 on v0

v1 whole, which is shorter than its diff:
```python
import math

import jax
import jax.numpy as jnp
from jax import lax
from jax.sharding import PartitionSpec as P

NDIR = 36
BOTH = ("spec", "geo")


def padded_2(cells, sides, width):
    for axis, dim in sides:
        count = lax.axis_size(axis)
        ends = count - 1
        head = lax.slice_in_dim(cells, 0, width, axis=dim)
        tail = lax.slice_in_dim(cells, cells.shape[dim] - width, cells.shape[dim], axis=dim)
        cells = jnp.concatenate(
            [
                lax.ppermute(tail, axis, [(i, (i + 1) % count) for i in range(ends)]),
                cells,
                lax.ppermute(head, axis, [((i + 1) % count, i) for i in range(ends)]),
            ],
            axis=dim,
        )
    return cells


def finish(energy_bf, transfer, wind_rows, wind_angle):
    energy = energy_bf.astype(jnp.float32)
    total = jnp.mean(energy, axis=1)
    ratio = total / (1.0 + total)
    component = jnp.arange(energy_bf.shape[1], dtype=jnp.int32)
    heading = 2.0 * math.pi * ((component % NDIR).astype(jnp.float32) + 0.5) / NDIR
    forcing = (
        0.3
        * wind_rows.astype(jnp.float32)[:, None]
        * jnp.maximum(jnp.cos(heading[None, :] - wind_angle.astype(jnp.float32)[:, None]), 0.0)
    )
    result = (
        energy * (1.0 + forcing - 0.5 * ratio[:, None])
        + 0.2 * transfer.astype(jnp.float32) / (1.0 + total)[:, None]
    )
    return result.astype(jnp.bfloat16)


def per_device(
    spectrum,
    sea_map,
    depth_factor,
    wind_speed,
    wind_dir,
    ice_mask,
    owner_map,
    pair_kernel,
    transfer_kernel,
):
    comp_dev, cells_x, cells_y = spectrum.shape
    spec_count = lax.axis_size("spec")
    geo_count = lax.axis_size("geo")
    cells_dev = cells_x * cells_y
    rows_dev = cells_dev // spec_count
    capacity = 2 * rows_dev // geo_count
    slot_count = geo_count * capacity
    width = ((comp_dev + 2 + 3) // 4) * 4

    masked = spectrum * sea_map.astype(jnp.bfloat16)[None, :, :]
    padded = padded_2(masked, (("geo", 1),), 1)
    extended = padded.astype(jnp.float32)
    component = lax.axis_index("spec") * comp_dev + jnp.arange(comp_dev, dtype=jnp.int32)
    frequency = (component // NDIR).astype(jnp.float32)
    heading = 2.0 * math.pi * ((component % NDIR).astype(jnp.float32) + 0.5) / NDIR
    cosine = jnp.cos(heading)[:, None, None]
    sine = jnp.sin(heading)[:, None, None]
    gain = (jnp.float32(1.1) ** (-0.5 * frequency))[:, None, None]
    sea_weight = sea_map.astype(jnp.float32)
    step_x = 0.7 * gain * jnp.abs(cosine) * depth_factor
    step_y = 0.7 * gain * jnp.abs(sine) * depth_factor
    centre = extended[:, 1:-1]
    west_side = extended[:, :-2]
    east_side = extended[:, 2:]
    zeros_y = jnp.zeros((comp_dev, cells_x, 1), jnp.float32)
    south_side = jnp.concatenate([zeros_y, centre[:, :, :-1]], axis=2)
    north_side = jnp.concatenate([centre[:, :, 1:], zeros_y], axis=2)
    upwind_x = jnp.where(cosine > 0, west_side, east_side)
    upwind_y = jnp.where(sine > 0, south_side, north_side)
    advected = centre - step_x * (centre - upwind_x) - step_y * (centre - upwind_y)
    propagated = (advected * sea_weight).astype(jnp.bfloat16)
    prop_cells = propagated.reshape(comp_dev, cells_dev).T

    owners = owner_map.reshape(spec_count, rows_dev)
    is_live = 1 - ice_mask.reshape(spec_count, rows_dev)
    onehot = (owners[:, :, None] == jnp.arange(geo_count, dtype=jnp.int32)[None, None, :]).astype(
        jnp.int32
    ) * is_live[:, :, None]
    before = jnp.cumsum(onehot, axis=1) - onehot
    position = jnp.sum(before * onehot, axis=2)
    block = jnp.arange(spec_count, dtype=jnp.int32)[:, None]
    send_row = jnp.where(
        is_live == 1, block * slot_count + owners * capacity + position, spec_count * slot_count
    ).reshape(cells_dev)
    row_total = spec_count * slot_count
    source = (
        jnp.full((row_total,), cells_dev, jnp.int32)
        .at[send_row]
        .set(jnp.arange(cells_dev, dtype=jnp.int32), mode="drop")
    )
    wind_pair = jnp.stack(
        [wind_speed.reshape(cells_dev), wind_dir.reshape(cells_dev)], axis=1
    ).astype(jnp.bfloat16)
    payload = jnp.concatenate(
        [
            prop_cells,
            wind_pair,
            jnp.zeros((cells_dev, width - comp_dev - 2), jnp.bfloat16),
        ],
        axis=1,
    )
    payload = jnp.concatenate([payload, jnp.zeros((1, width), jnp.bfloat16)], axis=0)
    outgoing = jnp.take(payload, source, axis=0)
    arrived = lax.all_to_all(outgoing, BOTH, split_axis=0, concat_axis=0, tiled=True)
    arrived = arrived.reshape(spec_count, slot_count, width)
    data = arrived[:, :, :comp_dev].transpose(1, 0, 2).reshape(slot_count, spec_count * comp_dev)
    wind_rows = arrived[0, :, comp_dev]
    wind_angle = arrived[0, :, comp_dev + 1]

    coupled = lax.dot_general(
        data, pair_kernel, (((1,), (1,)), ((), ())), preferred_element_type=jnp.float32
    )
    paired = (data.astype(jnp.float32) * coupled).astype(jnp.bfloat16)
    transfer = lax.dot_general(
        paired, transfer_kernel[0], (((1,), (1,)), ((), ())), preferred_element_type=jnp.float32
    ).astype(jnp.bfloat16)
    sourced = finish(data, transfer, wind_rows, wind_angle)

    back = sourced.reshape(slot_count, spec_count, comp_dev).transpose(1, 0, 2)
    back = jnp.concatenate(
        [back, jnp.zeros((spec_count, slot_count, width - comp_dev), jnp.bfloat16)], axis=2
    ).reshape(row_total, width)
    returned = lax.all_to_all(back, BOTH, split_axis=0, concat_axis=0, tiled=True)
    gather_row = jnp.minimum(send_row, row_total - 1)
    result_cells = jnp.take(returned, gather_row, axis=0)[:, :comp_dev]
    result_cells = jnp.where(is_live.reshape(cells_dev)[:, None] == 1, result_cells, prop_cells)
    return result_cells.T.reshape(comp_dev, cells_x, cells_y)


def solution(mesh):
    placed = (
        P("spec", "geo", None),
        P("geo", None),
        P("geo", None),
        P("geo", None),
        P("geo", None),
        P("geo", None),
        P("geo", None),
        P(),
        P("geo", None, None),
    )
    return jax.shard_map(
        per_device, mesh=mesh, in_specs=placed, out_specs=P("spec", "geo", None), check_vma=False
    )
```

time: 283 us -> 288 us (1.018)
  blocking collectives: 20.8 us -> 0 us
  local copies, waits for them, and re-layouts: 35 us -> 55.3 us
  starting transfers between devices: 39.3 us -> 27.6 us
  waiting for transfers between devices: 145 us -> 154 us
  other arithmetic: 12.6 us -> 19.6 us
    all_to_all x1 -> x0, blocking collectives: 20.8 us -> none  [per_device(): lax.all_to_all(result, 'spec', split_axis=0, concat_axis=1, tiled=True)]
    all_to_all x4 -> x2, starting transfers between devices: 32.2 us -> 20.8 us  [the longest x1 15.6 us: per_device(): lax.all_to_all(outgoing, BOTH, split_axis=0, concat_axis=0, tiled=True)]
    all_to_all x4 -> x2, waiting for transfers between devices: 145 us -> 154 us  [the longest x1 77.3 us: per_device(): lax.all_to_all(outgoing, BOTH, split_axis=0, concat_axis=0, tiled=True)]
    gather x6 -> x2, local copies, waits for them, and re-layouts: 18.3 us -> 26.1 us  [the longest x1 17 us: per_device(): outgoing = jnp.take(payload, source, axis=0)]
    all_to_all x6 -> x0, local copies, waits for them, and re-layouts: 6.43 us -> none  [the longest x4 2.99 us: per_device(): lax.all_to_all(flattened, 'spec', split_axis=1, concat_axis=0, tiled=True)]
    unnamed x14 -> x26, local copies, waits for them, and re-layouts: 0.03 us -> 5.99 us
    scatter x1, local copies, waits for them, and re-layouts: 2.44 us -> 8.06 us  [per_device(): source = jnp.full((row_total,), cells_dev, jnp.int32).at[send_row].set(jn...]
    transpose x0 -> x2, local copies, waits for them, and re-layouts: none -> 5.11 us  [per_device(): arrived[:, :, :comp_dev].transpose(1, 0, 2)]
  transfers between devices with their start and end apart: 6 -> 4, of which waited for: 3 -> 2; matrix products, arithmetic and copies ran while one was open for 7% -> 5% of each run, Pallas kernels for 0% -> 0%
where the time goes in v1:
time: 288 us; the launch traced here: 287 us
  waiting for transfers between devices  154 us (53%)
  local copies, waits for them, and re-layouts  55.3 us (19%)
  matrix products  30.4 us (11%)
  starting transfers between devices  27.6 us (10%)
  other arithmetic  19.6 us (7%)
    all_to_all x1, waiting for transfers between devices, per_device(): lax.all_to_all(outgoing, BOTH, split_axis=0, concat_axis=0, tiled=True)  77.3 us
    all_to_all x1, waiting for transfers between devices, per_device(): lax.all_to_all(back, BOTH, split_axis=0, concat_axis=0, tiled=True)  76.6 us
    dot_general x1, matrix products, per_device(): lax.dot_general(paired, transfer_kernel[0], (((1,), (1,)), ((), ())), pre...  22.4 us
    gather x1, local copies, waits for them, and re-layouts, per_device(): outgoing = jnp.take(payload, source, axis=0)  17 us
    all_to_all x1, starting transfers between devices, per_device(): lax.all_to_all(outgoing, BOTH, split_axis=0, concat_axis=0, tiled=True)  15.6 us
    gather x1, local copies, waits for them, and re-layouts, per_device(): result_cells = jnp.take(returned, gather_row, axis=0)[:, :comp_dev]  9.03 us
    scatter x1, local copies, waits for them, and re-layouts, per_device(): source = jnp.full((row_total,), cells_dev, jnp.int32).at[send_row].set(jn...  8.06 us
    dot_general x1, matrix products, per_device(): lax.dot_general(data, pair_kernel, (((1,), (1,)), ((), ())), preferred_el...  8.04 us
  transfers between devices with their start and end apart: 4, of which 2 were waited for; matrix products, arithmetic and copies ran while one was open for 5% of the time, Pallas kernels for 0%

profile of v1, /device:TPU:1, one launch (start us, length us, event | category | flops | bytes accessed | tf_op | source)
XLA Modules:
  0.0 287.3 jit_solution(2516355143012885737)
XLA Ops:
  0.8 1.7 copy_multiply_fusion
  2.5 4.9 %collective-permute-start = (bf16[324,1,128]{2,0,1:T(8,128)(2,1)S(1)}, bf16[324,1,128]{2,0,1:T(8,128)(2,1)S(1)}, u32[]{:S(2)}, u32[]{:S(2)}) collective-permute-start(bf16[324,1,128]{2,0,1:T(8,128)(2,1)S(1)} %get-tuple-element.13), channel_id=1, source_target_pairs={{0,1},{1,2},{2,3},{3,4},{4,5},{5,6},{6,7},{7,8},{8,9},{9,10},{10,1... | collective-permute-start | bytes 248840 | tf_op jit(solution)/shard_map/ppermute | solution.py:20
  7.4 1.9 collective-permute-start.1
  9.5 4.8 %reduce-window.6 = s32[4,64,4,128]{3,1,2,0:T(8,128)S(1)} reduce-window(s32[4,64,4,128]{3,1,2,0:T(8,128)S(1)} %fusion.12, s32[]{:T(128)} %constant.40.clone.1), window={size=1x1x1x128 pad=0_0x0_0x0_0x127_0}, to_apply=%region_0.1 | reduce-window | flops 16646144 | bytes 1048580 | tf_op jit(solution)/shard_map/reduce-window
  15.3 8.1 %scatter_custom_fusion = s32[4096]{0:T(1024)S(1)} fusion(s32[2048]{0:T(1024)S(1)} %bitcast.132, s32[2048]{0:T(1024)S(1)} %iota.32, s32[]{:T(128)} %constant.46.clone.1), kind=kCustom, calls=%fused_computation.55 | custom fusion | bytes 16388 | tf_op jit(solution)/shard_map/scatter | solution.py:106
  26.3 1.9 fusion.9
  30.3 1.8 maximum_maximum_fusion
  32.2 17.0 %gather_fusion = bf16[4096,328]{1,0:T(8,128)(2,1)} fusion(bf16[2049,328]{1,0:T(8,128)(2,1)S(1)} %concatenate.22, s32[4096]{0:T(1024)S(1)} %fusion.13), kind=kCustom, calls=%fused_computation | custom fusion | bytes 5390336 | tf_op jit(solution)/shard_map/jit(_take)/gather | solution.py:120
  49.3 3.5 %broadcast_select_fusion = bf16[256,16,328]{2,1,0:T(8,128)(2,1)} fusion(bf16[256,16,328]{2,1,0:T(8,128)(2,1)} %bitcast.112, pred[256,16]{1,0:T(8,128)(4,1)S(1)} %broadcast_in_dim.81), kind=kLoop, calls=%fused_computation.12 | loop fusion | flops 1343488 | bytes 5378048 | tf_op jit(solution)/shard_map/jit(_take)/select_n | solution.py:120
  52.7 15.6 %all-to-all-start = ((bf16[256,16,328]{2,1,0:T(8,128)(2,1)}), bf16[256,16,328]{2,1,0:T(8,128)(2,1)S(1)}, u32[]{:S(2)}, u32[]{:S(2)}) async-start(bf16[256,16,328]{2,1,0:T(8,128)(2,1)} %broadcast_select_fusion), calls=%async_computation | async-start | bytes 6291456 | tf_op jit(solution)/shard_map/all_to_all | solution.py:121
  68.3 77.3 %all-to-all-done = bf16[256,16,328]{2,1,0:T(8,128)(2,1)S(1)} async-done(((bf16[256,16,328]{2,1,0:T(8,128)(2,1)}), bf16[256,16,328]{2,1,0:T(8,128)(2,1)S(1)}, u32[]{:S(2)}, u32[]{:S(2)}) %all-to-all-start) | async-done | bytes 2687008 | tf_op jit(solution)/shard_map/all_to_all | solution.py:121
  145.6 2.0 slice_bitcast_fusion
  148.6 3.1 %copy.31 = bf16[1024,4,324]{0,2,1:T(8,128)(2,1)S(1)} copy(bf16[1024,4,324]{2,0,1:T(8,128)(2,1)} %slice_bitcast_fusion) | data formatting | bytes 5308416 | tf_op jit(solution)/shard_map/transpose | solution.py:123
  151.7 1.8 reshape.272
  153.5 8.0 %fusion.58 = bf16[1024,1296]{0,1:T(8,128)(2,1)S(1)} fusion(bf16[1024,1296]{0,1:T(8,128)(2,1)} %reshape.272, bf16[1296,1296]{1,0:T(8,128)(2,1)} %param.16), kind=kOutput, calls=%bitcast_fusion.1.clone.1 | convolution fusion | flops 3443834880 | bytes 8667648 | tf_op jit(solution)/shard_map/dot_general | solution.py:127
  161.6 22.4 %fusion.1 = bf16[1024,1296]{0,1:T(8,128)(2,1)S(1)} fusion(bf16[1024,1296]{0,1:T(8,128)(2,1)S(1)} %copy-done.1, bf16[1,1296,1296]{2,1,0:T(8,128)(2,1)S(1)} %copy-done.7, f32[1024]{0:T(1024)S(1)} %get-tuple-element.18, f32[1024]{0:T(1024)S(1)} %get-tuple-element.17, f32[1024]{0:T(1024)S(1)} %get-tuple-element.6, f32[1296]{0:T(1024)S(1)} %fusion.16, ...), kind=kOutput, calls=%fused_computation.7 | convolution fusion | flops 3457105920 | bytes 11343424 | tf_op jit(solution)/shard_map/dot_general | solution.py:131
  184.0 1.8 reshape.273
  185.8 3.3 %copy.34 = bf16[4,1024,324]{2,1,0:T(8,128)(2,1)S(1)} copy(bf16[4,1024,324]{1,2,0:T(8,128)(2,1)} %bitcast.114) | data formatting | bytes 5308416
  189.2 2.0 concatenate.23.clone
  191.2 5.2 %all-to-all-start.1 = ((bf16[256,16,328]{2,1,0:T(8,128)(2,1)}), bf16[256,16,328]{2,1,0:T(8,128)(2,1)S(1)}, u32[]{:S(2)}, u32[]{:S(2)}) async-start(bf16[256,16,328]{2,1,0:T(8,128)(2,1)} %bitcast.113), calls=%async_computation.1 | async-start | bytes 6291456 | tf_op jit(solution)/shard_map/all_to_all | solution.py:140
  196.4 76.6 %all-to-all-done.1 = bf16[256,16,328]{2,1,0:T(8,128)(2,1)S(1)} async-done(((bf16[256,16,328]{2,1,0:T(8,128)(2,1)}), bf16[256,16,328]{2,1,0:T(8,128)(2,1)S(1)}, u32[]{:S(2)}, u32[]{:S(2)}) %all-to-all-start.1) | async-done | bytes 2687008 | tf_op jit(solution)/shard_map/all_to_all | solution.py:140
  273.0 9.0 %gather_fusion.1 = bf16[2048,328]{1,0:T(8,128)(2,1)} fusion(bf16[4096,328]{1,0:T(8,128)(2,1)S(1)} %bitcast.107, s32[2048]{0:T(1024)S(1)} %broadcast_clamp_fusion), kind=kCustom, calls=%fused_computation.1 | custom fusion | bytes 2695168 | tf_op jit(solution)/shard_map/jit(_take)/gather | solution.py:142
  282.0 3.4 %fusion.10 = bf16[2048,324]{1,0:T(8,128)(2,1)S(1)} fusion(bf16[2048,328]{1,0:T(8,128)(2,1)} %gather_fusion.1, pred[2048]{0:T(1024)(128)(4,1)S(1)} %get-tuple-element.7, pred[2048]{0:T(1024)(128)(4,1)S(1)} %bitcast.131, bf16[324,16,128]{0,2,1:T(8,128)(2,1)} %copy-done), kind=kLoop, calls=%fused_computation.21 | loop fusion | flops 1327104 | bytes 3985408 | tf_op jit(solution)/shard_map/jit(_where)/select_n | solution.py:143
  285.4 1.9 copy.33
  (59 shorter events, 7.8 us)
Async XLA Ops:
  0.0 9.4 %copy-start.2 = (s32[16,128]{1,0:T(8,128)S(1)}, s32[16,128]{1,0:T(8,128)}, u32[]{:S(2)}) copy-start(s32[16,128]{1,0:T(8,128)} %param.15) | copy-start | bytes 24580
  0.0 9.4 %copy-start.3 = (s32[16,128]{1,0:T(8,128)S(1)}, s32[16,128]{1,0:T(8,128)}, u32[]{:S(2)}) copy-start(s32[16,128]{1,0:T(8,128)} %param.14) | copy-start | bytes 24580
  0.8 22.7 %copy-start.5 = (bf16[16,128]{1,0:T(8,128)(2,1)S(1)}, bf16[16,128]{1,0:T(8,128)(2,1)}, u32[]{:S(2)}) copy-start(bf16[16,128]{1,0:T(8,128)(2,1)} %param.12) | copy-start | bytes 12292
  0.8 23.0 %copy-start.6 = (bf16[16,128]{1,0:T(8,128)(2,1)S(1)}, bf16[16,128]{1,0:T(8,128)(2,1)}, u32[]{:S(2)}) copy-start(bf16[16,128]{1,0:T(8,128)(2,1)} %param.13) | copy-start | bytes 12292
  2.5 22.7 %collective-permute-start = (bf16[324,1,128]{2,0,1:T(8,128)(2,1)S(1)}, bf16[324,1,128]{2,0,1:T(8,128)(2,1)S(1)}, u32[]{:S(2)}, u32[]{:S(2)}) collective-permute-start(bf16[324,1,128]{2,0,1:T(8,128)(2,1)S(1)} %get-tuple-element.13), channel_id=1, source_target_pairs={{0,1},{1,2},{2,3},{3,4},{4,5},{5,6},{6,7},{7,8},{8,9},{9,10},{10,1... | collective-permute-start | bytes 248840 | tf_op jit(solution)/shard_map/ppermute | solution.py:20
  7.4 17.7 %collective-permute-start.1 = (bf16[324,1,128]{2,0,1:T(8,128)(2,1)S(1)}, bf16[324,1,128]{2,0,1:T(8,128)(2,1)S(1)}, u32[]{:S(2)}, u32[]{:S(2)}) collective-permute-start(bf16[324,1,128]{2,0,1:T(8,128)(2,1)S(1)} %get-tuple-element.14), channel_id=1, source_target_pairs={{1,0},{2,1},{3,2},{4,3},{5,4},{6,5},{7,6},{8,7},{9,8},{10,9},{11,1... | collective-permute-start | bytes 248840 | tf_op jit(solution)/shard_map/ppermute | solution.py:22
  25.4 0.9 copy-start.4
  29.1 1.2 copy-start
  52.7 92.9 %all-to-all-start = ((bf16[256,16,328]{2,1,0:T(8,128)(2,1)}), bf16[256,16,328]{2,1,0:T(8,128)(2,1)S(1)}, u32[]{:S(2)}, u32[]{:S(2)}) async-start(bf16[256,16,328]{2,1,0:T(8,128)(2,1)} %broadcast_select_fusion), calls=%async_computation | async-start | bytes 6291456 | tf_op jit(solution)/shard_map/all_to_all | solution.py:121
  153.5 8.1 %copy-start.1 = (bf16[1024,1296]{0,1:T(8,128)(2,1)S(1)}, bf16[1024,1296]{0,1:T(8,128)(2,1)}, u32[]{:S(2)}) copy-start(bf16[1024,1296]{0,1:T(8,128)(2,1)} %reshape.272) | copy-start | bytes 7962628
  153.5 8.1 %copy-start.7 = (bf16[1,1296,1296]{2,1,0:T(8,128)(2,1)S(1)}, bf16[1,1296,1296]{2,1,0:T(8,128)(2,1)}, u32[]{:S(2)}) copy-start(bf16[1,1296,1296]{2,1,0:T(8,128)(2,1)} %param.17) | copy-start | bytes 10077700
  191.2 81.8 %all-to-all-start.1 = ((bf16[256,16,328]{2,1,0:T(8,128)(2,1)}), bf16[256,16,328]{2,1,0:T(8,128)(2,1)S(1)}, u32[]{:S(2)}, u32[]{:S(2)}) async-start(bf16[256,16,328]{2,1,0:T(8,128)(2,1)} %bitcast.113), calls=%async_computation.1 | async-start | bytes 6291456 | tf_op jit(solution)/shard_map/all_to_all | solution.py:140

commit v2 on v1

--- a/solution.py
+++ b/solution.py
@@ -32,11 +32,12 @@
     ratio = total / (1.0 + total)
     component = jnp.arange(energy_bf.shape[1], dtype=jnp.int32)
     heading = 2.0 * math.pi * ((component % NDIR).astype(jnp.float32) + 0.5) / NDIR
-    forcing = (
-        0.3
-        * wind_rows.astype(jnp.float32)[:, None]
-        * jnp.maximum(jnp.cos(heading[None, :] - wind_angle.astype(jnp.float32)[:, None]), 0.0)
+    angle = wind_angle.astype(jnp.float32)
+    alignment = (
+        jnp.cos(heading)[None, :] * jnp.cos(angle)[:, None]
+        + jnp.sin(heading)[None, :] * jnp.sin(angle)[:, None]
     )
+    forcing = 0.3 * wind_rows.astype(jnp.float32)[:, None] * jnp.maximum(alignment, 0.0)
     result = (
         energy * (1.0 + forcing - 0.5 * ratio[:, None])
         + 0.2 * transfer.astype(jnp.float32) / (1.0 + total)[:, None]
@@ -86,38 +87,33 @@
     upwind_y = jnp.where(sine > 0, south_side, north_side)
     advected = centre - step_x * (centre - upwind_x) - step_y * (centre - upwind_y)
     propagated = (advected * sea_weight).astype(jnp.bfloat16)
-    prop_cells = propagated.reshape(comp_dev, cells_dev).T
+    flat = propagated.reshape(comp_dev, cells_dev)
 
     owners = owner_map.reshape(spec_count, rows_dev)
     is_live = 1 - ice_mask.reshape(spec_count, rows_dev)
     onehot = (owners[:, :, None] == jnp.arange(geo_count, dtype=jnp.int32)[None, None, :]).astype(
-        jnp.int32
-    ) * is_live[:, :, None]
-    before = jnp.cumsum(onehot, axis=1) - onehot
-    position = jnp.sum(before * onehot, axis=2)
-    block = jnp.arange(spec_count, dtype=jnp.int32)[:, None]
-    send_row = jnp.where(
-        is_live == 1, block * slot_count + owners * capacity + position, spec_count * slot_count
-    ).reshape(cells_dev)
+        jnp.float32
+    ) * is_live[:, :, None].astype(jnp.float32)
+    lower = (
+        jnp.arange(rows_dev, dtype=jnp.int32)[None, :] < jnp.arange(rows_dev, dtype=jnp.int32)[:, None]
+    ).astype(jnp.bfloat16)
+    before = jnp.einsum(
+        "ij,bjo->bio", lower, onehot.astype(jnp.bfloat16), preferred_element_type=jnp.float32
+    )
+    position = jnp.sum(before * onehot, axis=2).astype(jnp.int32)
+    slot = jnp.where(is_live == 1, owners * capacity + position, -1)
+    route = (
+        jnp.arange(slot_count, dtype=jnp.int32)[None, :, None] == slot[:, None, :]
+    ).astype(jnp.bfloat16)
+    wind_pair = jnp.stack([wind_speed.reshape(cells_dev), wind_dir.reshape(cells_dev)], axis=0)
+    payload = jnp.concatenate(
+        [flat, wind_pair, jnp.zeros((width - comp_dev - 2, cells_dev), jnp.bfloat16)], axis=0
+    ).reshape(width, spec_count, rows_dev)
+    outgoing = jnp.einsum(
+        "bki,cbi->bkc", route, payload, preferred_element_type=jnp.float32
+    ).astype(jnp.bfloat16)
     row_total = spec_count * slot_count
-    source = (
-        jnp.full((row_total,), cells_dev, jnp.int32)
-        .at[send_row]
-        .set(jnp.arange(cells_dev, dtype=jnp.int32), mode="drop")
-    )
-    wind_pair = jnp.stack(
-        [wind_speed.reshape(cells_dev), wind_dir.reshape(cells_dev)], axis=1
-    ).astype(jnp.bfloat16)
-    payload = jnp.concatenate(
-        [
-            prop_cells,
-            wind_pair,
-            jnp.zeros((cells_dev, width - comp_dev - 2), jnp.bfloat16),
-        ],
-        axis=1,
-    )
-    payload = jnp.concatenate([payload, jnp.zeros((1, width), jnp.bfloat16)], axis=0)
-    outgoing = jnp.take(payload, source, axis=0)
+    outgoing = outgoing.reshape(row_total, width)
     arrived = lax.all_to_all(outgoing, BOTH, split_axis=0, concat_axis=0, tiled=True)
     arrived = arrived.reshape(spec_count, slot_count, width)
     data = arrived[:, :, :comp_dev].transpose(1, 0, 2).reshape(slot_count, spec_count * comp_dev)
@@ -138,10 +134,13 @@
         [back, jnp.zeros((spec_count, slot_count, width - comp_dev), jnp.bfloat16)], axis=2
     ).reshape(row_total, width)
     returned = lax.all_to_all(back, BOTH, split_axis=0, concat_axis=0, tiled=True)
-    gather_row = jnp.minimum(send_row, row_total - 1)
-    result_cells = jnp.take(returned, gather_row, axis=0)[:, :comp_dev]
-    result_cells = jnp.where(is_live.reshape(cells_dev)[:, None] == 1, result_cells, prop_cells)
-    return result_cells.T.reshape(comp_dev, cells_x, cells_y)
+    returned = returned.reshape(spec_count, slot_count, width)[:, :, :comp_dev]
+    placed_back = jnp.einsum(
+        "bkc,bki->cbi", returned, route, preferred_element_type=jnp.float32
+    ).astype(jnp.bfloat16).reshape(comp_dev, cells_dev)
+    live_flat = is_live.reshape(cells_dev)[None, :] == 1
+    result = jnp.where(live_flat, placed_back, flat)
+    return result.reshape(comp_dev, cells_x, cells_y)
 
 
 def solution(mesh):

time: 288 us -> 241 us (0.84)
  blocking collectives: 0 us -> 81.6 us
  waiting for transfers between devices: 154 us -> 81.2 us
  local copies, waits for them, and re-layouts: 55.3 us -> 23.5 us
  matrix products: 30.4 us -> 21.5 us
  other arithmetic: 19.6 us -> 10.8 us
  starting transfers between devices: 27.6 us -> 21 us
    all_to_all x0 -> x1, blocking collectives: none -> 81.6 us  [per_device(): lax.all_to_all(back, BOTH, split_axis=0, concat_axis=0, tiled=True)]
    all_to_all x1 -> x0, waiting for transfers between devices: 76.6 us -> none  [per_device(): lax.all_to_all(back, BOTH, split_axis=0, concat_axis=0, tiled=True)]
    gather x2 -> x0, local copies, waits for them, and re-layouts: 26.1 us -> none  [the longest x1 17 us: per_device(): outgoing = jnp.take(payload, source, axis=0)]
    scatter x1 -> x0, local copies, waits for them, and re-layouts: 8.06 us -> none  [per_device(): source = jnp.full((row_total,), cells_dev, jnp.int32).at[send_row].set(jn...]
    dot_general x1, matrix products: 22.4 us -> 15.2 us  [per_device(): lax.dot_general(paired, transfer_kernel[0], (((1,), (1,)), ((), ())), pre...]
    select_n x4 -> x2, other arithmetic: 6.9 us -> 1.21 us  [the longest x1 1.2 us: per_device(): result = jnp.where(live_flat, placed_back, flat)]
    convert_element_type x1 -> x3, local copies, waits for them, and re-layouts: 0.85 us -> 6.31 us  [the longest x1 4.56 us: per_device(): outgoing = jnp.einsum('bki,cbi->bkc', route, payload, preferred_element_t...]
    all_to_all x1 -> x0, starting transfers between devices: 5.19 us -> none  [per_device(): lax.all_to_all(back, BOTH, split_axis=0, concat_axis=0, tiled=True)]
  transfers between devices with their start and end apart: 4 -> 3, of which waited for: 2 -> 2; matrix products, arithmetic and copies ran while one was open for 5% -> 0% of each run, Pallas kernels for 0% -> 0%
where the time goes in v2:
time: 241 us; the launch traced here: 240 us
  blocking collectives  81.6 us (34%)
  waiting for transfers between devices  81.2 us (34%)
  local copies, waits for them, and re-layouts  23.5 us (10%)
  matrix products  21.5 us (9%)
  starting transfers between devices  21 us (9%)
  other arithmetic  10.8 us (4%)
    all_to_all x1, blocking collectives, per_device(): lax.all_to_all(back, BOTH, split_axis=0, concat_axis=0, tiled=True)  81.6 us
    all_to_all x1, waiting for transfers between devices, per_device(): lax.all_to_all(outgoing, BOTH, split_axis=0, concat_axis=0, tiled=True)  77.3 us
    dot_general x1, matrix products, per_device(): lax.dot_general(paired, transfer_kernel[0], (((1,), (1,)), ((), ())), pre...  15.2 us
    all_to_all x1, starting transfers between devices, per_device(): lax.all_to_all(outgoing, BOTH, split_axis=0, concat_axis=0, tiled=True)  14.1 us
    transpose x2, local copies, waits for them, and re-layouts, per_device(): arrived[:, :, :comp_dev].transpose(1, 0, 2)  5.1 us
    ppermute x1, starting transfers between devices, padded_2(): lax.ppermute(tail, axis, [(i, (i + 1) % count) for i in range(ends)])  4.94 us
  transfers between devices with their start and end apart: 3, of which 2 were waited for; matrix products, arithmetic and copies ran while one was open for 0% of the time, Pallas kernels for 0%

profile of v2, /device:TPU:1, one launch (start us, length us, event | category | flops | bytes accessed | tf_op | source)
XLA Modules:
  0.0 240.0 jit_solution(2957318850500000419)
XLA Ops:
  0.0 0.8 fusion.60
  0.8 1.4 broadcast_multiply_fusion
  2.5 4.9 %collective-permute-start = (bf16[324,1,128]{2,1,0:T(2,128)(2,1)S(1)}, bf16[324,1,128]{2,1,0:T(2,128)(2,1)S(1)}, u32[]{:S(2)}, u32[]{:S(2)}) collective-permute-start(bf16[324,1,128]{2,1,0:T(2,128)(2,1)S(1)} %get-tuple-element.10), channel_id=1, source_target_pairs={{0,1},{1,2},{2,3},{3,4},{4,5},{5,6},{6,7},{7,8},{8,9},{9,10},{10,1... | collective-permute-start | bytes 248840 | tf_op jit(solution)/shard_map/ppermute | solution.py:20
  7.4 1.9 collective-permute-start.1
  10.1 4.0 %collective-permute-done.1 = bf16[324,1,128]{2,1,0:T(2,128)(2,1)S(1)} collective-permute-done((bf16[324,1,128]{2,1,0:T(2,128)(2,1)S(1)}, bf16[324,1,128]{2,1,0:T(2,128)(2,1)S(1)}, u32[]{:S(2)}, u32[]{:S(2)}) %collective-permute-start.1) | collective-permute-done | bytes 82976 | tf_op jit(solution)/shard_map/ppermute | solution.py:22
  14.1 1.0 maximum_convert_fusion
  15.1 1.0 fusion.58
  16.1 2.8 %fusion.14 = bf16[324,16,128]{2,1,0:T(8,128)(2,1)S(1)} fusion(f32[324,18,128]{2,1,0:T(8,128)S(1)} %maximum_convert_fusion, f32[324,16,127]{2,1,0:T(8,128)S(1)} %get-tuple-element.9, f32[324,16,127]{2,1,0:T(8,128)S(1)} %get-tuple-element.8, f32[16,128]{1,0:T(8,128)S(1)} %get-tuple-element.12, f32[324]{0:T(512)S(1)} %get-tuple-element.16, ...), kind=kLoop, calls=%fused_computation.21 | loop fusion | flops 7962624 | bytes 14576296 | tf_op jit(solution)/shard_map/convert_element_type | solution.py:89
  19.8 3.7 %fusion.15 = bf16[4,1024,328]{1,2,0:T(8,128)(2,1)} fusion(s32[4,512]{1,0:T(4,128)S(1)} %add_select_fusion.1, bf16[1,4,512]{2,0,1:T(2,128)(2,1)S(1)} %concatenate.31, bf16[1,4,512]{2,0,1:T(2,128)(2,1)S(1)} %concatenate.30, bf16[324,4,512]{2,0,1:T(8,128)(2,1)S(1)} %copy.18, bf16[328]{0:T(512)(128)(2,1)S(1)} %pad.6.clone), kind=kOutput, calls=%fused_computation.22 | convolution fusion | flops 1384546304 | bytes 4031120 | tf_op jit(solution)/shard_map/bki,cbi->bkc/dot_general | solution.py:112
  23.5 4.6 %copy.21 = bf16[4,1024,328]{2,1,0:T(8,128)(2,1)} copy(bf16[4,1024,328]{1,2,0:T(8,128)(2,1)} %fusion.15) | data formatting | bytes 5373952 | tf_op jit(solution)/shard_map/convert_element_type | solution.py:114
  28.1 14.1 %all-to-all-start = ((bf16[256,16,328]{2,1,0:T(8,128)(2,1)}), bf16[256,16,328]{2,1,0:T(8,128)(2,1)S(1)}, u32[]{:S(2)}, u32[]{:S(2)}) async-start(bf16[256,16,328]{2,1,0:T(8,128)(2,1)} %bitcast.41), calls=%async_computation | async-start | bytes 6291456 | tf_op jit(solution)/shard_map/all_to_all | solution.py:117
  42.3 77.3 %all-to-all-done = bf16[256,16,328]{2,1,0:T(8,128)(2,1)S(1)} async-done(((bf16[256,16,328]{2,1,0:T(8,128)(2,1)}), bf16[256,16,328]{2,1,0:T(8,128)(2,1)S(1)}, u32[]{:S(2)}, u32[]{:S(2)}) %all-to-all-start) | async-done | bytes 2687008 | tf_op jit(solution)/shard_map/all_to_all | solution.py:117
  119.6 2.8 %multiply_reduce_fusion = (f32[1024]{0:T(1024)S(1)}, f32[1024]{0:T(1024)S(1)}, f32[1024]{0:T(1024)S(1)}) fusion(bf16[4,1024,328]{2,1,0:T(8,128)(2,1)S(1)} %bitcast.38), kind=kLoop, calls=%fused_computation.45 | loop fusion | flops 3072 | bytes 16384 | tf_op jit(solution)/shard_map/mul | solution.py:40
  122.9 2.0 slice_bitcast_fusion
  124.9 3.1 %copy.22 = bf16[1024,4,324]{0,2,1:T(8,128)(2,1)S(1)} copy(bf16[1024,4,324]{2,0,1:T(8,128)(2,1)} %slice_bitcast_fusion) | data formatting | bytes 5308416 | tf_op jit(solution)/shard_map/transpose | solution.py:119
  128.0 1.8 reshape.179
  129.8 15.2 %fusion.3 = bf16[1024,1296]{0,1:T(8,128)(2,1)S(1)} fusion(bf16[1024,1296]{0,1:T(8,128)(2,1)} %reshape.179, bf16[1,1296,1296]{2,1,0:T(8,128)(2,1)} %param.17, f32[1024]{0:T(1024)S(1)} %get-tuple-element.15, f32[1024]{0:T(1024)S(1)} %get-tuple-element.14, f32[1024]{0:T(1024)S(1)} %get-tuple-element.6, f32[1296]{0:T(1024)S(1)} %get-tuple-element.20, ...), kind=kOutput, calls=%fused_computation.7 | convolution fusion | flops 6903595008 | bytes 12057728 | tf_op jit(solution)/shard_map/dot_general | solution.py:127
  145.1 1.8 reshape.180
  146.9 3.3 %copy.27 = bf16[4,1024,324]{2,1,0:T(8,128)(2,1)S(1)} copy(bf16[4,1024,324]{1,2,0:T(8,128)(2,1)} %bitcast.43) | data formatting | bytes 5308416
  150.6 81.6 %all_to_all.18 = bf16[256,16,328]{2,1,0:T(8,128)(2,1)S(1)} all-to-all(bf16[256,16,328]{2,1,0:T(8,128)(2,1)S(1)} %bitcast.42), channel_id=1, replica_groups=mesh['spec'=4,'geo'=64] {'spec','geo'}, dimensions={0} | all-to-all | bytes 5373952 | tf_op jit(solution)/shard_map/all_to_all | solution.py:136
  232.2 2.2 fusion.19
  234.4 1.7 copy.25
  236.2 2.6 %reshape.182 = bf16[324,16,128]{2,1,0:T(8,128)(2,1)S(1)} reshape(bf16[324,4,512]{2,1,0:T(4,128)(2,1)} %copy.25) | data formatting | bytes 2654208 | tf_op jit(solution)/shard_map/reshape | solution.py:140
  238.8 1.2 broadcast_select_fusion
  (35 shorter events, 2.7 us)
Async XLA Ops:
  0.0 9.4 %copy-start.2 = (s32[16,128]{1,0:T(8,128)S(1)}, s32[16,128]{1,0:T(8,128)}, u32[]{:S(2)}) copy-start(s32[16,128]{1,0:T(8,128)} %param.14) | copy-start | bytes 24580
  0.0 9.5 %copy-start.4 = (s32[16,128]{1,0:T(8,128)S(1)}, s32[16,128]{1,0:T(8,128)}, u32[]{:S(2)}) copy-start(s32[16,128]{1,0:T(8,128)} %param.15) | copy-start | bytes 24580
  0.0 9.5 %copy-start.5 = (bf16[16,128]{1,0:T(8,128)(2,1)S(1)}, bf16[16,128]{1,0:T(8,128)(2,1)}, u32[]{:S(2)}) copy-start(bf16[16,128]{1,0:T(8,128)(2,1)} %param.12) | copy-start | bytes 12292
  0.0 9.5 %copy-start.6 = (bf16[16,128]{1,0:T(8,128)(2,1)S(1)}, bf16[16,128]{1,0:T(8,128)(2,1)}, u32[]{:S(2)}) copy-start(bf16[16,128]{1,0:T(8,128)(2,1)} %param.13) | copy-start | bytes 12292
  2.5 7.6 %collective-permute-start = (bf16[324,1,128]{2,1,0:T(2,128)(2,1)S(1)}, bf16[324,1,128]{2,1,0:T(2,128)(2,1)S(1)}, u32[]{:S(2)}, u32[]{:S(2)}) collective-permute-start(bf16[324,1,128]{2,1,0:T(2,128)(2,1)S(1)} %get-tuple-element.10), channel_id=1, source_target_pairs={{0,1},{1,2},{2,3},{3,4},{4,5},{5,6},{6,7},{7,8},{8,9},{9,10},{10,1... | collective-permute-start | bytes 248840 | tf_op jit(solution)/shard_map/ppermute | solution.py:20
  7.4 6.7 %collective-permute-start.1 = (bf16[324,1,128]{2,1,0:T(2,128)(2,1)S(1)}, bf16[324,1,128]{2,1,0:T(2,128)(2,1)S(1)}, u32[]{:S(2)}, u32[]{:S(2)}) collective-permute-start(bf16[324,1,128]{2,1,0:T(2,128)(2,1)S(1)} %get-tuple-element.11), channel_id=1, source_target_pairs={{1,0},{2,1},{3,2},{4,3},{5,4},{6,5},{7,6},{8,7},{9,8},{10,9},{11,1... | collective-permute-start | bytes 248840 | tf_op jit(solution)/shard_map/ppermute | solution.py:22
  15.1 1.0 copy-start.3
  19.0 4.6 %copy-start = (bf16[324,16,128]{2,1,0:T(8,128)(2,1)}, bf16[324,16,128]{2,1,0:T(8,128)(2,1)S(1)}, u32[]{:S(2)}) copy-start(bf16[324,16,128]{2,1,0:T(8,128)(2,1)S(1)} %fusion.14) | copy-start | bytes 3981316
  28.1 91.5 %all-to-all-start = ((bf16[256,16,328]{2,1,0:T(8,128)(2,1)}), bf16[256,16,328]{2,1,0:T(8,128)(2,1)S(1)}, u32[]{:S(2)}, u32[]{:S(2)}) async-start(bf16[256,16,328]{2,1,0:T(8,128)(2,1)} %bitcast.41), calls=%async_computation | async-start | bytes 6291456 | tf_op jit(solution)/shard_map/all_to_all | solution.py:117
  234.4 4.4 %copy-start.1 = (bf16[324,16,128]{2,1,0:T(8,128)(2,1)S(1)}, bf16[324,16,128]{2,1,0:T(8,128)(2,1)}, u32[]{:S(2)}) copy-start(bf16[324,16,128]{2,1,0:T(8,128)(2,1)} %copy-done) | copy-start | bytes 3981316
